TPU v7x, 32 devices: a whole 2x2x4 slice. The times are simulated.
32 devices in a mesh: dp: 8 (over z, y), tensor: 4 (over x, core).
Axes of the slice: x: 2, y: 2, z: 4, core: 2. Of those that a mesh axis runs over, the one named last changes fastest.
Arguments:
- tokens: bfloat16 [32768, 768], P(('dp', 'tensor')), may hold values from -6 to 6
- segment_ids: int32 [16, 2048], P('dp'), may hold values from 0 to 15, never falling along the last dimension, each value on 1 to 1024 neighbouring positions
- qkv_weight: bfloat16 [768, 3, 768], P('dp', None, 'tensor'), may hold values from -0.21875 to 0.21875
- qv_bias: bfloat16 [2, 768], P(None, 'tensor'), may hold values from -2 to 2
- out_weight: bfloat16 [768, 768], P('dp', 'tensor'), may hold values from -0.4375 to 0.4375
- out_bias: bfloat16 [768], replicated, may hold values from -2 to 2
- first_gain: bfloat16 [768], replicated, may hold values from 0.25 to 1.75
- first_shift: bfloat16 [768], replicated, may hold values from -2 to 2
- up_weight: bfloat16 [768, 3072], P('dp', 'tensor'), may hold values from -0.21875 to 0.21875
- up_bias: bfloat16 [3072], P('tensor'), may hold values from -3 to 3
- down_weight: bfloat16 [768, 3072], P('dp', 'tensor'), may hold values from -0.109375 to 0.109375
- down_bias: bfloat16 [768], replicated, may hold values from -2 to 2
- second_gain: bfloat16 [768], replicated, may hold values from 0.25 to 1.75
- second_shift: bfloat16 [768], replicated, may hold values from -2 to 2
- output_grad: bfloat16 [32768, 768], P(('dp', 'tensor')), may hold values from -6 to 6
Outputs:
- output: bfloat16 [32768, 768], P(('dp', 'tensor'))
- input_grad: float32 [32768, 768], P(('dp', 'tensor'))
- qkv_grad: float32 [768, 3, 768], P('dp', None, 'tensor')
- qv_bias_grad: float32 [2, 768], P(None, 'tensor')
- out_weight_grad: float32 [768, 768], P('dp', 'tensor')
- up_weight_grad: float32 [768, 3072], P('dp', 'tensor')
- up_bias_grad: float32 [3072], P('tensor')
- down_weight_grad: float32 [768, 3072], P('dp', 'tensor')
- vector_grads: float32 [6, 768], replicated
Inputs may be any that keep to these rules, and one draw needn't show every extreme that they name: `segment_ids`: document ids never fall along a sequence; each document has at most 1024 tokens.
All inputs are finite; a program needn't handle non-finite values.
Results may differ from a plain program's by a relative error of at most 0.015.
Values may be sent and summed in bfloat16 or wider, within the bound.
No kernel may reach another device: no remote copies, remote signals or barrier semaphores. Data moves between devices by JAX's collectives and lax.ppermute only.
A program may use at most 192 MiB of HBM per device.

v0:
```python
from functools import partial
import jax
import jax.numpy as jnp
from jax import lax
from jax.sharding import PartitionSpec as P

HEAD_DIM = 64
EPSILON = 1e-12
MASKED = -1e30


def matmul_plain(left, right):
    return jnp.dot(left, right, preferred_element_type=jnp.float32)


def times_transposed(left, right):
    return lax.dot_general(
        left, right, (((1,), (1,)), ((), ())), preferred_element_type=jnp.float32
    )


def over_rows(left, right):
    return lax.dot_general(
        left, right, (((0,), (0,)), ((), ())), preferred_element_type=jnp.float32
    )


def normalize(values, gain, shift):
    center = jnp.mean(values, axis=-1, keepdims=True)
    offset = values - center
    spread = jnp.mean(offset * offset, axis=-1, keepdims=True)
    inverse = lax.rsqrt(spread + EPSILON)
    normed = offset * inverse
    return (normed * gain + shift, normed, inverse)


def normalize_back(incoming, normed, inverse, gain):
    weighted = incoming * gain
    centered = weighted - jnp.mean(weighted, axis=-1, keepdims=True)
    centered = centered - normed * jnp.mean(weighted * normed, axis=-1, keepdims=True)
    return (centered * inverse, jnp.sum(incoming * normed, axis=0), jnp.sum(incoming, axis=0))


def masked_scores(query_rows, seg_rows, key_seq, seg_seq):
    scores = jnp.einsum(
        "qhd,khd->hqk", query_rows, key_seq, preferred_element_type=jnp.float32
    ) * HEAD_DIM ** (-0.5)
    same_doc = (seg_rows[:, None] == seg_seq[None, :])[None]
    return jnp.where(same_doc, scores, MASKED)


def attend_forward(query_seq, key_seq, value_seq, seg_seq, block_rows):
    block_count = query_seq.shape[0] // block_rows

    def one_block(block_index):
        first_row = block_index * block_rows
        query_rows = lax.dynamic_slice_in_dim(query_seq, first_row, block_rows, 0)
        seg_rows = lax.dynamic_slice_in_dim(seg_seq, first_row, block_rows, 0)
        scores = masked_scores(query_rows, seg_rows, key_seq, seg_seq)
        row_max = jnp.max(scores, axis=-1, keepdims=True)
        powers = jnp.exp(scores - row_max)
        row_total = jnp.sum(powers, axis=-1, keepdims=True)
        weights = (powers / row_total).astype(jnp.bfloat16)
        context = jnp.einsum("hqk,khd->qhd", weights, value_seq, preferred_element_type=jnp.float32)
        return (context, (row_max + jnp.log(row_total))[..., 0])

    contexts, log_sums = lax.map(one_block, jnp.arange(block_count, dtype=jnp.int32))
    return (contexts.reshape(query_seq.shape), log_sums)


def attend_backward(query_seq, key_seq, value_seq, seg_seq, log_sums, grad_seq, block_rows):
    block_count = query_seq.shape[0] // block_rows
    score_scale = HEAD_DIM ** (-0.5)

    def one_block(running, block_index):
        key_grad, value_grad = running
        first_row = block_index * block_rows
        query_rows = lax.dynamic_slice_in_dim(query_seq, first_row, block_rows, 0)
        seg_rows = lax.dynamic_slice_in_dim(seg_seq, first_row, block_rows, 0)
        grad_rows = lax.dynamic_slice_in_dim(grad_seq, first_row, block_rows, 0)
        scores = masked_scores(query_rows, seg_rows, key_seq, seg_seq)
        probs = jnp.exp(scores - log_sums[block_index][..., None])
        weights = probs.astype(jnp.bfloat16)
        prob_grad = jnp.einsum(
            "qhd,khd->hqk", grad_rows, value_seq, preferred_element_type=jnp.float32
        )
        inner = jnp.sum(probs * prob_grad, axis=-1, keepdims=True)
        score_grad = (probs * (prob_grad - inner)).astype(jnp.bfloat16)
        query_grad = (
            jnp.einsum("hqk,khd->qhd", score_grad, key_seq, preferred_element_type=jnp.float32)
            * score_scale
        )
        key_grad = (
            key_grad
            + jnp.einsum("hqk,qhd->khd", score_grad, query_rows, preferred_element_type=jnp.float32)
            * score_scale
        )
        value_grad = value_grad + jnp.einsum(
            "hqk,qhd->khd", weights, grad_rows, preferred_element_type=jnp.float32
        )
        return ((key_grad, value_grad), query_grad)

    empty_grad = jnp.zeros(key_seq.shape, jnp.float32)
    (key_grad, value_grad), query_grads = lax.scan(
        one_block, (empty_grad, empty_grad), jnp.arange(block_count, dtype=jnp.int32)
    )
    return (query_grads.reshape(query_seq.shape), key_grad, value_grad)


def local(
    tokens,
    segment_ids,
    qkv_weight,
    qv_bias,
    out_weight,
    out_bias,
    first_gain,
    first_shift,
    up_weight,
    up_bias,
    down_weight,
    down_bias,
    second_gain,
    second_shift,
    output_grad,
):
    row_count, model_width = tokens.shape
    sequences, seq_length = segment_ids.shape
    block_rows = min(512, seq_length)
    gathered = lax.all_gather(tokens, "tensor", axis=0, tiled=True)
    qkv_full, out_full, up_full, down_full = (
        lax.all_gather(qkv_weight, "dp", axis=0, tiled=True),
        lax.all_gather(out_weight, "dp", axis=0, tiled=True),
        lax.all_gather(up_weight, "dp", axis=0, tiled=True),
        lax.all_gather(down_weight, "dp", axis=0, tiled=True),
    )
    local_width = qkv_full.shape[2]
    shape_four = (sequences, seq_length, local_width // HEAD_DIM, HEAD_DIM)
    qkv_flat = qkv_full.reshape(model_width, 3 * local_width)
    bias_pair = qv_bias.astype(jnp.float32)
    projected = matmul_plain(gathered, qkv_flat)
    queries = (projected[:, :local_width] + bias_pair[0]).astype(jnp.bfloat16).reshape(shape_four)
    keys_all = projected[:, local_width : 2 * local_width].astype(jnp.bfloat16).reshape(shape_four)
    values_all = (
        (projected[:, 2 * local_width :] + bias_pair[1]).astype(jnp.bfloat16).reshape(shape_four)
    )

    def forward_sequence(packed):
        return attend_forward(packed[0], packed[1], packed[2], packed[3], block_rows)

    contexts, log_sums = lax.map(forward_sequence, (queries, keys_all, values_all, segment_ids))
    context = contexts.reshape(-1, local_width).astype(jnp.bfloat16)
    attended = lax.psum_scatter(
        times_transposed(context, out_full), "tensor", scatter_dimension=0, tiled=True
    )
    gain_one = first_gain.astype(jnp.float32)
    gain_two = second_gain.astype(jnp.float32)
    first, normed_one, inverse_one = normalize(
        tokens.astype(jnp.float32) + attended + out_bias.astype(jnp.float32),
        gain_one,
        first_shift.astype(jnp.float32),
    )
    first_low = first.astype(jnp.bfloat16)
    spread_rows = lax.all_gather(first_low, "tensor", axis=0, tiled=True)
    up_used, down_used = (up_full, down_full)
    hidden_bias = up_bias.astype(jnp.float32)
    hidden_pre = matmul_plain(spread_rows, up_used) + hidden_bias
    activated, gelu_back = jax.vjp(partial(jax.nn.gelu, approximate=False), hidden_pre)
    act_low = activated.astype(jnp.bfloat16)
    fed = lax.psum_scatter(
        times_transposed(
            lax.slice_in_dim(act_low, 0, lax.axis_size("tensor") * row_count, axis=0), down_used
        ).astype(jnp.bfloat16),
        "tensor",
        scatter_dimension=0,
        tiled=True,
    ).astype(jnp.float32)
    second, normed_two, inverse_two = normalize(
        first + fed + down_bias.astype(jnp.float32), gain_two, second_shift.astype(jnp.float32)
    )
    output = second.astype(jnp.bfloat16)
    grad_second, gain_two_g, shift_two_g = normalize_back(
        output_grad.astype(jnp.float32), normed_two, inverse_two, gain_two
    )
    fed_low = grad_second.astype(jnp.bfloat16)
    down_bias_g = jnp.sum(fed_low.astype(jnp.float32), axis=0)
    fed_rows = lax.all_gather(fed_low, "tensor", axis=0, tiled=True)
    act_grad = matmul_plain(fed_rows, down_used)
    pre_grad = gelu_back(act_grad)[0].astype(jnp.bfloat16)
    down_grad = over_rows(fed_rows, act_low)
    up_grad = over_rows(spread_rows, pre_grad)
    up_bias_g = jnp.sum(pre_grad.astype(jnp.float32), axis=0)
    first_grad = lax.psum_scatter(
        times_transposed(pre_grad, up_used).astype(jnp.bfloat16),
        "tensor",
        scatter_dimension=0,
        tiled=True,
    ).astype(jnp.float32)
    grad_first, gain_one_g, shift_one_g = normalize_back(
        grad_second + first_grad, normed_one, inverse_one, gain_one
    )
    attn_low = grad_first.astype(jnp.bfloat16)
    out_bias_g = jnp.sum(attn_low.astype(jnp.float32), axis=0)
    attn_rows = lax.all_gather(attn_low, "tensor", axis=0, tiled=True)
    context_grad = matmul_plain(attn_rows, out_full).astype(jnp.bfloat16).reshape(shape_four)
    out_weight_g = over_rows(attn_rows, context)

    def backward_sequence(packed):
        return attend_backward(
            packed[0], packed[1], packed[2], packed[3], packed[4], packed[5], block_rows
        )

    query_g, key_g, value_g = lax.map(
        backward_sequence, (queries, keys_all, values_all, segment_ids, log_sums, context_grad)
    )
    mixed_grad = jnp.concatenate(
        [
            query_g.reshape(-1, local_width),
            key_g.reshape(-1, local_width),
            value_g.reshape(-1, local_width),
        ],
        axis=1,
    ).astype(jnp.bfloat16)
    qkv_g = over_rows(gathered, mixed_grad).reshape(model_width, 3, local_width)
    mixed_wide = mixed_grad.astype(jnp.float32)
    qv_g = jnp.stack(
        [
            jnp.sum(mixed_wide[:, :local_width], axis=0),
            jnp.sum(mixed_wide[:, 2 * local_width :], axis=0),
        ]
    )
    input_grad = grad_first + lax.psum_scatter(
        times_transposed(mixed_grad, qkv_flat).astype(jnp.bfloat16),
        "tensor",
        scatter_dimension=0,
        tiled=True,
    ).astype(jnp.float32)
    qkv_share, out_share, up_share, down_share = (
        lax.psum_scatter(qkv_g, "dp", scatter_dimension=0, tiled=True),
        lax.psum_scatter(out_weight_g, "dp", scatter_dimension=0, tiled=True),
        lax.psum_scatter(up_grad, "dp", scatter_dimension=0, tiled=True),
        lax.psum_scatter(down_grad, "dp", scatter_dimension=0, tiled=True),
    )
    qv_share, up_bias_share = lax.psum((qv_g, up_bias_g), "dp")
    vectors = lax.psum(
        jnp.stack([out_bias_g, gain_one_g, shift_one_g, down_bias_g, gain_two_g, shift_two_g]),
        ("dp", "tensor"),
    )
    return (
        output,
        input_grad,
        qkv_share,
        qv_share,
        out_share,
        up_share,
        up_bias_share,
        down_share,
        vectors,
    )


def solution(mesh):
    in_specs = (
        P(("dp", "tensor"), None),
        P("dp", None),
        P("dp", None, "tensor"),
        P(None, "tensor"),
        P("dp", "tensor"),
        P(),
        P(),
        P(),
        P("dp", "tensor"),
        P("tensor"),
        P("dp", "tensor"),
        P(),
        P(),
        P(),
        P(("dp", "tensor"), None),
    )
    out_specs = (
        P(("dp", "tensor"), None),
        P(("dp", "tensor"), None),
        P("dp", None, "tensor"),
        P(None, "tensor"),
        P("dp", "tensor"),
        P("dp", "tensor"),
        P("tensor"),
        P("dp", "tensor"),
        P(),
    )
    return jax.shard_map(local, mesh=mesh, in_specs=in_specs, out_specs=out_specs, check_vma=False)
```

profile of v0, /device:TPU:0, one launch (start us, length us, event | category | flops | bytes accessed | tf_op | source)
XLA Modules:
  0.0 1469.7 jit_solution(13262983610031420961)
XLA Ops:
  9.9 38.8 %all_gather.25 = bf16[768,3,192]{2,1,0:T(4,128)(2,1)S(1)} all-gather(bf16[96,3,192]{2,1,0:T(4,128)(2,1)S(1)} %copy.55), channel_id=1, replica_groups=mesh['dp'=8,'tensor'=4] {'dp'}, dimensions={0}, use_global_device_ids=true | all-gather | bytes 995328 | tf_op jit(solution)/shard_map/all_gather | solution.py:132
  49.6 33.1 %all_gather.26 = bf16[768,192]{1,0:T(8,128)(2,1)} all-gather(bf16[96,192]{1,0:T(8,128)(2,1)S(1)} %copy-done.24), channel_id=1, replica_groups=mesh['dp'=8,'tensor'=4] {'dp'}, dimensions={0}, use_global_device_ids=true | all-gather | bytes 331776 | tf_op jit(solution)/shard_map/all_gather | solution.py:133
  109.5 194.5 %while.54 = (s32[]{:T(128)}, bf16[2,2048,3,64]{3,2,1,0:T(4,128)(2,1)}, f32[2,4,3,512]{3,2,1,0:T(4,128)S(1)}, bf16[2,2048,3,64]{1,3,2,0:T(8,128)(2,1)}, s32[2,204...) while((s32[]{:T(128)}, ...), condition=%wide.region_5.6_spmd, body=%wide.region_0.5_spmd.sunk | while | flops 844102144 | bytes 53436884 | solution.py:151
  113.1 90.5 %while.57 = (s32[]{:T(128)}, bf16[4,512,3,64]{1,3,2,0:T(8,128)(2,1)S(1)}, f32[4,3,512]{2,1,0:T(4,128)S(1)}, s32[4]{0:T(128)S(1)}, s32[2048]{0:T(1024)S(1)}, /*in...) while((s32[]{:T(128)}, ...), condition=%wide.region_4.4_spmd, body=%wide.region_1.3_spmd.sunk | while | flops 844102144 | bytes 44179652 | solution.py:67
  115.1 7.1 fusion.128
  122.2 6.8 fusion.129
  129.0 6.7 fusion.130
  137.7 7.1 fusion.128
  144.8 6.8 fusion.129
  151.6 6.7 fusion.130
  160.3 7.1 fusion.128
  167.5 6.8 fusion.129
  174.2 6.7 fusion.130
  182.9 7.1 fusion.128
  190.1 6.8 fusion.129
  196.8 6.7 fusion.130
  210.4 90.5 %while.57 = (s32[]{:T(128)}, bf16[4,512,3,64]{1,3,2,0:T(8,128)(2,1)S(1)}, f32[4,3,512]{2,1,0:T(4,128)S(1)}, s32[4]{0:T(128)S(1)}, s32[2048]{0:T(1024)S(1)}, /*in...) while((s32[]{:T(128)}, ...), condition=%wide.region_4.4_spmd, body=%wide.region_1.3_spmd.sunk | while | flops 844102144 | bytes 44179652 | solution.py:67
  212.3 7.1 fusion.128
  219.5 6.8 fusion.129
  226.2 6.7 fusion.130
  235.0 7.1 fusion.128
  242.1 6.8 fusion.129
  248.9 6.7 fusion.130
  257.6 7.1 fusion.128
  264.7 6.8 fusion.129
  271.5 6.7 fusion.130
  280.2 7.1 fusion.128
  287.4 6.8 fusion.129
  294.1 6.7 fusion.130
  304.0 9.9 copy.60
  315.8 6.4 fusion.59
  322.9 97.6 %reduce-scatter.9.cloned.1.call-done = f32[1024,768]{1,0:T(8,128)} async-done(((f32[4096,768]{1,0:T(8,128)}), f32[1024,768]{1,0:T(8,128)}) %reduce-scatter.9.cloned.1.call-update) | async-done | bytes 3145744 | tf_op jit(solution)/shard_map/reduce_scatter | solution.py:153
  426.3 45.7 %all-gather.9.cloned.1.call-done = bf16[4096,768]{1,0:T(8,128)(2,1)} async-done(((bf16[1024,768]{1,0:T(8,128)(2,1)}), bf16[4096,768]{1,0:T(8,128)(2,1)}) %all-gather.9.cloned.1.call-update) | async-done | bytes 6291472 | tf_op jit(solution)/shard_map/all_gather | solution.py:164
  471.9 34.8 %multiply_convert_fusion.1 = (bf16[4096,768]{1,0:T(8,128)(2,1)}, f32[4096,768]{1,0:T(8,128)}, f32[4096,768]{1,0:T(8,128)}) fusion(f32[768]{0:T(1024)S(1)} %convert_element_type.114, bf16[4096,768]{1,0:T(8,128)(2,1)} %all-gather.9.cloned.1.call-done, bf16[768,768]{1,0:T(8,128)(2,1)} %all-gather.11.cloned.1.call-done), kind=kOutput, calls=%fused_computation.62 | convolution fusion | flops 5039456256 | bytes 38931456 | tf_op jit(solution)/shard_map/dot_general | solution.py:13
  506.8 8.8 all-gather.13.cloned.1.call-done
  515.5 9.1 convolution_convert_fusion.2
  525.4 56.1 %reduce-scatter.11.cloned.1.call-done = bf16[1024,768]{1,0:T(8,128)(2,1)} async-done(((bf16[4096,768]{1,0:T(8,128)(2,1)}), bf16[1024,768]{1,0:T(8,128)(2,1)}) %reduce-scatter.11.cloned.1.call-update) | async-done | bytes 1572880 | tf_op jit(solution)/shard_map/reduce_scatter | solution.py:170
  591.3 46.3 %all-gather.15.cloned.1.call-done = bf16[4096,768]{1,0:T(8,128)(2,1)} async-done(((bf16[1024,768]{1,0:T(8,128)(2,1)}), bf16[4096,768]{1,0:T(8,128)(2,1)}) %all-gather.15.cloned.1.call-update) | async-done | bytes 6291472 | tf_op jit(solution)/shard_map/all_gather | solution.py:187
  637.6 19.0 %convert_reduce_fusion = (f32[768]{0:T(1024)}, bf16[4096,768]{1,0:T(8,128)(2,1)}) fusion(f32[4096,768]{1,0:T(8,128)} %get-tuple-element.390, f32[4096,768]{1,0:T(8,128)} %get-tuple-element.406, f32[768]{0:T(1024)S(1)} %convert_element_type.114, bf16[4096,768]{1,0:T(8,128)(2,1)} %all-gather.15.cloned.1.call-done, ...), kind=kOutput, calls=%fused_computation.60 | convolution fusion | flops 4885314560 | bytes 38934528 | tf_op jit(solution)/shard_map/dot_general | solution.py:13
  656.6 9.7 convolution_convert_fusion.1
  666.4 58.5 %reduce-scatter.13.cloned.1.call-done = bf16[1024,768]{1,0:T(8,128)(2,1)} async-done(((bf16[4096,768]{1,0:T(8,128)(2,1)}), bf16[1024,768]{1,0:T(8,128)(2,1)}) %reduce-scatter.13.cloned.1.call-update) | async-done | bytes 1572880 | tf_op jit(solution)/shard_map/reduce_scatter | solution.py:193
  732.6 46.3 %all-gather.17.cloned.1.call-done = bf16[4096,768]{1,0:T(8,128)(2,1)} async-done(((bf16[1024,768]{1,0:T(8,128)(2,1)}), bf16[4096,768]{1,0:T(8,128)(2,1)}) %all-gather.17.cloned.1.call-update) | async-done | bytes 6291472 | tf_op jit(solution)/shard_map/all_gather | solution.py:204
  789.7 301.7 %while.56 = (s32[]{:T(128)}, bf16[2,2048,3,64]{3,2,1,0:T(4,128)(2,1)}, bf16[2,2048,3,64]{1,3,2,0:T(8,128)(2,1)}, bf16[2,2048,3,64]{1,3,2,0:T(8,128)(2,1)}, bf16[...) while((s32[]{:T(128)}, ...), condition=%wide.region_21.22_spmd, body=%wide.region_17.21_spmd.sunk | while | flops 2063563264 | bytes 193981360 | solution.py:213
  797.1 132.6 %while.58 = (s32[]{:T(128)}, f32[2048,3,64]{0,2,1:T(8,128)}, f32[2048,3,64]{0,2,1:T(8,128)}, bf16[4,512,3,64]{1,3,2,0:T(8,128)(2,1)}, s32[4]{0:T(128)S(1)}, /*in...) while((s32[]{:T(128)}, f32[2048,3,64]{0,2,1:T(8,128)}, ...), condition=%wide.region_20.20_spmd.clone, body=%wide.region_18.19_spmd.clone.sunk | while | flops 2063563264 | bytes 156690960 | solution.py:104
  813.6 6.2 multiply_convert_fusion.3
  846.0 6.2 multiply_convert_fusion.3
  879.8 6.2 multiply_convert_fusion.3
  913.7 6.2 multiply_convert_fusion.3
  947.8 132.6 %while.58 = (s32[]{:T(128)}, f32[2048,3,64]{0,2,1:T(8,128)}, f32[2048,3,64]{0,2,1:T(8,128)}, bf16[4,512,3,64]{1,3,2,0:T(8,128)(2,1)}, s32[4]{0:T(128)S(1)}, /*in...) while((s32[]{:T(128)}, f32[2048,3,64]{0,2,1:T(8,128)}, ...), condition=%wide.region_20.20_spmd.clone, body=%wide.region_18.19_spmd.clone.sunk | while | flops 2063563264 | bytes 156690960 | solution.py:104
  964.2 6.2 multiply_convert_fusion.3
  996.6 6.2 multiply_convert_fusion.3
  1030.5 6.2 multiply_convert_fusion.3
  1064.4 6.2 multiply_convert_fusion.3
  1095.1 9.7 copy.67
  1111.7 7.0 convolution_convert_fusion
  1118.7 10.1 fusion.62
  1128.9 11.2 fusion.63
  1146.0 7.5 fusion.60
  1155.7 41.0 %psum.23 = f32[6,768]{1,0:T(8,128)} all-reduce(f32[6,768]{1,0:T(8,128)S(1)} %stack.39), channel_id=1, replica_groups=mesh['dp'=8,'tensor'=4] {'dp','tensor'}, use_global_device_ids=true, to_apply=%region_38.39 | all-reduce | flops 4608 | bytes 36864 | tf_op jit(solution)/shard_map/psum | solution.py:245
  1201.0 22.6 %all-reduce = (f32[2,192]{1,0:T(2,128)}, f32[768]{0:T(1024)}) all-reduce(f32[2,192]{1,0:T(2,128)S(1)} %pad_maximum_fusion, f32[768]{0:T(1024)S(1)} %copy-done.31), channel_id=1, replica_groups=mesh['dp'=8,'tensor'=4] {'dp'}, use_global_device_ids=true, to_apply=%region_26.27 | all-reduce | flops 1152 | bytes 9216 | tf_op jit(solution)/shard_map/psum | solution.py:244
  1227.0 24.6 %reduce-scatter.21.cloned.1.call-done = f32[96,768]{1,0:T(8,128)} async-done(((f32[768,768]{1,0:T(8,128)}), f32[96,768]{1,0:T(8,128)}) %reduce-scatter.21.cloned.1.call-update) | async-done | bytes 294928 | tf_op jit(solution)/shard_map/reduce_scatter | solution.py:241
  1251.6 72.4 %reduce-scatter.23.cloned.1.call-done = f32[96,768]{1,0:T(8,128)} async-done(((f32[768,768]{1,0:T(8,128)}), f32[96,768]{1,0:T(8,128)}) %reduce-scatter.23.cloned.1.call-update) | async-done | bytes 294928 | tf_op jit(solution)/shard_map/reduce_scatter | solution.py:242
  1324.1 65.9 %reduce-scatter.19.cloned.1.call-done = f32[96,192]{1,0:T(8,128)} async-done(((f32[768,192]{1,0:T(8,128)}), f32[96,192]{1,0:T(8,128)}) %reduce-scatter.19.cloned.1.call-update) | async-done | bytes 73744 | tf_op jit(solution)/shard_map/reduce_scatter | solution.py:240
  1390.0 71.9 %reduce-scatter.17.cloned.1.call-done = f32[96,3,192]{2,0,1:T(8,128)} async-done(((f32[768,3,192]{2,0,1:T(8,128)}), f32[96,3,192]{2,0,1:T(8,128)}) %reduce-scatter.17.cloned.1.call-update) | async-done | bytes 221200 | tf_op jit(solution)/shard_map/reduce_scatter | solution.py:239
  (444 shorter events, 346.7 us)
Async XLA Ops:
  8.0 41.6 %copy-start.24 = (bf16[96,192]{1,0:T(8,128)(2,1)S(1)}, bf16[96,192]{1,0:T(8,128)(2,1)}, u32[]{:S(2)}) copy-start(bf16[96,192]{1,0:T(8,128)(2,1)} %param.27) | copy-start | bytes 110596
  8.0 74.7 %copy-start.32 = (bf16[2,192]{1,0:T(2,128)(2,1)S(1)}, bf16[2,192]{1,0:T(2,128)(2,1)}, u32[]{:S(2)}) copy-start(bf16[2,192]{1,0:T(2,128)(2,1)} %param.26) | copy-start | bytes 2308
  8.0 74.7 %all-gather.7.cloned.1.call-start = ((), (), s32[]{:S(2)}) async-start(), calls=%async_computation.8 | async-start | bytes 7864320 | tf_op jit(solution)/shard_map/all_gather | solution.py:130
  8.8 411.7 %reduce-scatter.9.cloned.1.call-start = ((), (), s32[]{:S(2)}) async-start(), calls=%async_computation.9 | async-start | bytes 15728640 | tf_op jit(solution)/shard_map/reduce_scatter | solution.py:153
  49.6 33.2 %copy-start.20 = (bf16[768,3,192]{0,2,1:T(8,128)(2,1)}, bf16[768,3,192]{0,2,1:T(8,128)(2,1)S(1)}, u32[]{:S(2)}) copy-start(bf16[768,3,192]{0,2,1:T(8,128)(2,1)S(1)} %copy.56) | copy-start | bytes 2654212
  103.6 5.9 copy-start.23
  304.0 18.2 %copy-start.22 = (f32[2,4,3,512]{3,2,1,0:T(4,128)}, f32[2,4,3,512]{3,2,1,0:T(4,128)S(1)}, u32[]{:S(2)}) copy-start(f32[2,4,3,512]{3,2,1,0:T(4,128)S(1)} %get-tuple-element.826) | copy-start | bytes 147460
  304.0 11.7 copy-start.16
  322.2 104.0 %all-gather.11.cloned.1.call-start = ((), (), s32[]{:S(2)}) async-start(), calls=%async_computation.11 | async-start | bytes 1327104 | tf_op jit(solution)/shard_map/all_gather | solution.py:134
  322.8 149.1 %all-gather.9.cloned.1.call-start = ((), (), s32[]{:S(2)}) async-start(), calls=%async_computation.10 | async-start | bytes 7864320 | tf_op jit(solution)/shard_map/all_gather | solution.py:164
  425.6 90.0 %all-gather.13.cloned.1.call-start = ((), (), s32[]{:S(2)}) async-start(), calls=%async_computation.12 | async-start | bytes 1327104 | tf_op jit(solution)/shard_map/all_gather | solution.py:135
  426.2 155.4 %reduce-scatter.11.cloned.1.call-start = ((), (), s32[]{:S(2)}) async-start(), calls=%async_computation.13 | async-start | bytes 7864320 | tf_op jit(solution)/shard_map/reduce_scatter | solution.py:170
  524.7 112.9 %all-gather.15.cloned.1.call-start = ((), (), s32[]{:S(2)}) async-start(), calls=%async_computation.14 | async-start | bytes 7864320 | tf_op jit(solution)/shard_map/all_gather | solution.py:187
  591.3 133.6 %reduce-scatter.13.cloned.1.call-start = ((), (), s32[]{:S(2)}) async-start(), calls=%async_computation.15 | async-start | bytes 7864320 | tf_op jit(solution)/shard_map/reduce_scatter | solution.py:193
  637.6 19.0 %copy-start.40 = (bf16[768,768]{1,0:T(8,128)(2,1)S(1)}, bf16[768,768]{1,0:T(8,128)(2,1)}, u32[]{:S(2)}) copy-start(bf16[768,768]{1,0:T(8,128)(2,1)} %all-gather.11.cloned.1.call-done) | copy-start | bytes 3538948
  666.4 112.5 %all-gather.17.cloned.1.call-start = ((), (), s32[]{:S(2)}) async-start(), calls=%async_computation.16 | async-start | bytes 7864320 | tf_op jit(solution)/shard_map/all_gather | solution.py:204
  729.0 49.9 %copy-start.17 = (bf16[768,192]{1,0:T(8,128)(2,1)S(1)}, bf16[768,192]{1,0:T(8,128)(2,1)}, u32[]{:S(2)}) copy-start(bf16[768,192]{1,0:T(8,128)(2,1)} %all_gather.26) | copy-start | bytes 884740
  732.5 491.1 %reduce-scatter.15.cloned.1.call-start = ((), (), s32[]{:S(2)}) async-start(), calls=%async_computation.17 | async-start | bytes 7864320 | tf_op jit(solution)/shard_map/reduce_scatter | solution.py:232
  797.2 6.0 copy-start.2
  797.2 6.0 copy-start.5
  797.2 6.0 copy-start.7
  819.8 5.8 copy-start
  819.8 5.8 copy-start.6
  828.1 5.9 copy-start.2
  828.1 5.9 copy-start.5
  828.1 5.9 copy-start.7
  852.2 5.8 copy-start
  852.2 5.8 copy-start.6
  862.0 5.9 copy-start.2
  862.0 5.9 copy-start.5
  862.0 5.9 copy-start.7
  886.1 5.8 copy-start
  886.1 5.8 copy-start.6
  895.9 5.9 copy-start.2
  895.9 5.9 copy-start.5
  895.9 6.0 copy-start.7
  929.7 7.2 copy-start.4
  929.7 7.2 copy-start.18
  947.8 6.0 copy-start.2
  947.8 6.0 copy-start.5
  947.8 6.0 copy-start.7
  970.5 5.8 copy-start
  970.5 5.8 copy-start.6
  978.8 5.9 copy-start.2
  978.8 5.9 copy-start.5
  978.8 5.9 copy-start.7
  1002.8 5.8 copy-start
  1002.8 5.8 copy-start.6
  1012.7 5.9 copy-start.2
  1012.7 5.9 copy-start.5
  1012.7 5.9 copy-start.7
  1036.7 5.8 copy-start
  1036.7 5.8 copy-start.6
  1046.5 5.9 copy-start.2
  1046.5 5.9 copy-start.5
  1046.5 6.0 copy-start.7
  1080.4 7.1 copy-start.4
  1080.4 7.1 copy-start.18
  1118.7 133.0 %reduce-scatter.21.cloned.1.call-start = ((), (), s32[]{:S(2)}) async-start(), calls=%async_computation.20 | async-start | bytes 2654208 | tf_op jit(solution)/shard_map/reduce_scatter | solution.py:241
  1128.8 11.3 copy-start.13
  1128.8 195.2 %reduce-scatter.23.cloned.1.call-start = ((), (), s32[]{:S(2)}) async-start(), calls=%async_computation.21 | async-start | bytes 2654208 | tf_op jit(solution)/shard_map/reduce_scatter | solution.py:242
  1140.1 249.9 %reduce-scatter.19.cloned.1.call-start = ((), (), s32[]{:S(2)}) async-start(), calls=%async_computation.19 | async-start | bytes 884736 | tf_op jit(solution)/shard_map/reduce_scatter | solution.py:240
  1146.0 316.0 %reduce-scatter.17.cloned.1.call-start = ((), (), s32[]{:S(2)}) async-start(), calls=%async_computation.18 | async-start | bytes 2654208 | tf_op jit(solution)/shard_map/reduce_scatter | solution.py:239
  1200.4 23.3 %copy-start.10 = (f32[1024,768]{1,0:T(8,128)S(1)}, f32[1024,768]{1,0:T(8,128)}, u32[]{:S(2)}) copy-start(f32[1024,768]{1,0:T(8,128)} %get-tuple-element.384) | copy-start | bytes 9437188
  (50 other events, 135.7 us)
Sparse Core Ops, SparseCore 0:
  10.4 49.0 all-gather.6
  322.3 98.1 reduce-scatter.8
  666.5 58.3 reduce-scatter.12
Sparse Core Ops, SparseCore 1:
  324.9 40.5 all-gather.10
  425.7 46.2 all-gather.8
  474.0 41.5 all-gather.12
  524.8 56.7 reduce-scatter.10
  591.4 46.2 all-gather.14
  732.6 46.2 all-gather.16
  1118.8 58.9 reduce-scatter.14
  1182.0 69.5 reduce-scatter.20
  1256.0 68.0 reduce-scatter.22
  1328.3 61.6 reduce-scatter.18
  1393.9 68.0 reduce-scatter.16
where the time goes:
time: 1480 us; the launch traced here: 1470 us
  waiting for transfers between devices  596 us (40%)
  matrix products  424 us (29%)
  other arithmetic  146 us (10%)
  blocking collectives  135 us (9%)
  local copies, waits for them, and re-layouts  122 us (8%)
  loops' own time  27.8 us (2%)
  between operations  16.6 us (1%)
    reduce_scatter x1, waiting for transfers between devices, local(): lax.psum_scatter(times_transposed(context, out_full), 'tensor', scatter_d...  97.6 us
    reduce_scatter x1, waiting for transfers between devices, local(): lax.psum_scatter(down_grad, 'dp', scatter_dimension=0, tiled=True)  72.4 us
    reduce_scatter x1, waiting for transfers between devices, local(): lax.psum_scatter(qkv_g, 'dp', scatter_dimension=0, tiled=True)  71.9 us
    dot_general x16, matrix products, masked_scores(): jnp.einsum('qhd,khd->hqk', query_rows, key_seq, preferred_element_type=jn...  71.9 us
    reduce_scatter x1, waiting for transfers between devices, local(): lax.psum_scatter(out_weight_g, 'dp', scatter_dimension=0, tiled=True)  65.9 us
    dot_general x4, matrix products, matmul_plain(): return jnp.dot(left, right, preferred_element_type=jnp.float32)  64.8 us
    reduce_scatter x1, waiting for transfers between devices, local(): lax.psum_scatter(times_transposed(pre_grad, up_used).astype(jnp.bfloat16)...  58.5 us
    reduce_scatter x1, waiting for transfers between devices, local(): lax.psum_scatter(times_transposed(lax.slice_in_dim(act_low, 0, lax.axis_s...  56.1 us
  transfers between devices with their start and end apart: 14, of which 11 were waited for; matrix products, arithmetic and copies ran while one was open for 6% of the time, Pallas kernels for 0%

commit v1 on v0

--- a/solution.py
+++ b/solution.py
@@ -184,7 +184,14 @@
     )
     fed_low = grad_second.astype(jnp.bfloat16)
     down_bias_g = jnp.sum(fed_low.astype(jnp.float32), axis=0)
-    fed_rows = lax.all_gather(fed_low, "tensor", axis=0, tiled=True)
+    ring = [fed_low]
+    for hop in range(3):
+        ring.append(lax.ppermute(ring[-1], "tensor", [(dev, (dev + 1) % 4) for dev in range(4)]))
+    fed_rows = jnp.roll(
+        jnp.concatenate(ring[::-1], axis=0),
+        (lax.axis_index("tensor") + 1) * ring[0].shape[0],
+        axis=0,
+    )
     act_grad = matmul_plain(fed_rows, down_used)
     pre_grad = gelu_back(act_grad)[0].astype(jnp.bfloat16)
     down_grad = over_rows(fed_rows, act_low)

time: 1480 us -> 1590 us (1.074)
  matrix products: 424 us -> 498 us
    ppermute x0 -> x3, waiting for transfers between devices: none -> 59.9 us  [local(): lax.ppermute(ring[-1], 'tensor', [(dev, (dev + 1) % 4) for dev in range(4)])]
    reduce_scatter x1, waiting for transfers between devices: 72.4 us -> 24.6 us  [local(): lax.psum_scatter(down_grad, 'dp', scatter_dimension=0, tiled=True)]
    reduce_scatter x1, waiting for transfers between devices: 24.6 us -> 72.4 us  [local(): lax.psum_scatter(up_grad, 'dp', scatter_dimension=0, tiled=True)]
    all_gather x1 -> x0, waiting for transfers between devices: 46.3 us -> none  [local(): fed_rows = lax.all_gather(fed_low, 'tensor', axis=0, tiled=True)]
    dot_general x16, matrix products: 71.9 us -> 108 us  [masked_scores(): jnp.einsum('qhd,khd->hqk', query_rows, key_seq, preferred_element_type=jn...]
    dot_general x8, matrix products: 46 us -> 80.2 us  [one_block(): jnp.einsum('hqk,qhd->khd', weights, grad_rows, preferred_element_type=jnp...]
    dot_general x8, matrix products: 46.5 us -> 16.2 us  [one_block(): jnp.einsum('hqk,khd->qhd', score_grad, key_seq, preferred_element_type=jn...]
    dot_general x8, matrix products: 28.8 us -> 46.3 us  [one_block(): jnp.einsum('hqk,qhd->khd', score_grad, query_rows, preferred_element_type...]
  transfers between devices with their start and end apart: 14 -> 16, of which waited for: 11 -> 13; matrix products, arithmetic and copies ran while one was open for 6% -> 5% of each run, Pallas kernels for 0% -> 0%
where the time goes in v1:
time: 1590 us; the launch traced here: 1570 us
  waiting for transfers between devices  610 us (38%)
  matrix products  498 us (31%)
  other arithmetic  153 us (10%)
  blocking collectives  136 us (9%)
  local copies, waits for them, and re-layouts  133 us (8%)
  loops' own time  27.8 us (2%)
  between operations  16.5 us (1%)
    dot_general x16, matrix products, masked_scores(): jnp.einsum('qhd,khd->hqk', query_rows, key_seq, preferred_element_type=jn...  108 us
    reduce_scatter x1, waiting for transfers between devices, local(): lax.psum_scatter(times_transposed(context, out_full), 'tensor', scatter_d...  97.6 us
    dot_general x8, matrix products, one_block(): jnp.einsum('hqk,qhd->khd', weights, grad_rows, preferred_element_type=jnp...  80.2 us
    reduce_scatter x1, waiting for transfers between devices, local(): lax.psum_scatter(up_grad, 'dp', scatter_dimension=0, tiled=True)  72.4 us
    reduce_scatter x1, waiting for transfers between devices, local(): lax.psum_scatter(qkv_g, 'dp', scatter_dimension=0, tiled=True)  72.2 us
    reduce_scatter x1, waiting for transfers between devices, local(): lax.psum_scatter(out_weight_g, 'dp', scatter_dimension=0, tiled=True)  65.7 us
    dot_general x4, matrix products, matmul_plain(): return jnp.dot(left, right, preferred_element_type=jnp.float32)  64.1 us
    dot_general x8, matrix products, one_block(): jnp.einsum('qhd,khd->hqk', grad_rows, value_seq, preferred_element_type=j...  63.3 us
  transfers between devices with their start and end apart: 16, of which 13 were waited for; matrix products, arithmetic and copies ran while one was open for 5% of the time, Pallas kernels for 0%

profile of v1, /device:TPU:0, one launch (start us, length us, event | category | flops | bytes accessed | tf_op | source)
XLA Modules:
  0.0 1574.7 jit_solution(4783129928843045149)
XLA Ops:
  9.9 38.8 %all_gather.22 = bf16[768,3,192]{2,1,0:T(4,128)(2,1)S(1)} all-gather(bf16[96,3,192]{2,1,0:T(4,128)(2,1)S(1)} %copy.55), channel_id=1, replica_groups=mesh['dp'=8,'tensor'=4] {'dp'}, dimensions={0}, use_global_device_ids=true | all-gather | bytes 995328 | tf_op jit(solution)/shard_map/all_gather | solution.py:132
  49.6 33.1 %all_gather.23 = bf16[768,192]{1,0:T(8,128)(2,1)} all-gather(bf16[96,192]{1,0:T(8,128)(2,1)S(1)} %copy-done.29), channel_id=1, replica_groups=mesh['dp'=8,'tensor'=4] {'dp'}, dimensions={0}, use_global_device_ids=true | all-gather | bytes 331776 | tf_op jit(solution)/shard_map/all_gather | solution.py:133
  109.4 194.2 %while.54 = (s32[]{:T(128)}, bf16[2,2048,3,64]{3,2,1,0:T(4,128)(2,1)}, f32[2,4,3,512]{3,2,1,0:T(4,128)S(1)}, bf16[2,2048,3,64]{1,3,2,0:T(8,128)(2,1)}, s32[2,204...) while((s32[]{:T(128)}, ...), condition=%wide.region_5.6_spmd, body=%wide.region_0.5_spmd.sunk | while | flops 844102144 | bytes 53437376 | solution.py:151
  113.1 90.3 %while.57 = (s32[]{:T(128)}, bf16[4,512,3,64]{1,3,2,0:T(8,128)(2,1)S(1)}, f32[4,3,512]{2,1,0:T(4,128)S(1)}, s32[4]{0:T(128)S(1)}, s32[2048]{0:T(1024)S(1)}, /*in...) while((s32[]{:T(128)}, ...), condition=%wide.region_4.4_spmd, body=%wide.region_1.3_spmd.sunk | while | flops 844102144 | bytes 44179644 | solution.py:67
  115.1 7.1 fusion.133
  122.2 6.8 fusion.134
  137.6 7.1 fusion.133
  144.7 6.8 fusion.134
  160.2 7.1 fusion.133
  167.3 6.8 fusion.134
  182.8 7.1 fusion.133
  189.9 6.8 fusion.134
  210.2 90.3 %while.57 = (s32[]{:T(128)}, bf16[4,512,3,64]{1,3,2,0:T(8,128)(2,1)S(1)}, f32[4,3,512]{2,1,0:T(4,128)S(1)}, s32[4]{0:T(128)S(1)}, s32[2048]{0:T(1024)S(1)}, /*in...) while((s32[]{:T(128)}, ...), condition=%wide.region_4.4_spmd, body=%wide.region_1.3_spmd.sunk | while | flops 844102144 | bytes 44179644 | solution.py:67
  212.2 7.1 fusion.133
  219.2 6.8 fusion.134
  234.7 7.1 fusion.133
  241.8 6.8 fusion.134
  257.3 7.1 fusion.133
  264.4 6.8 fusion.134
  279.9 7.1 fusion.133
  303.6 10.0 copy.60
  322.6 97.6 %reduce-scatter.9.cloned.1.call-done = f32[1024,768]{1,0:T(8,128)} async-done(((f32[4096,768]{1,0:T(8,128)}), f32[1024,768]{1,0:T(8,128)}) %reduce-scatter.9.cloned.1.call-update) | async-done | bytes 3145744 | tf_op jit(solution)/shard_map/reduce_scatter | solution.py:153
  425.9 45.7 %all-gather.8.cloned.1.call-done = bf16[4096,768]{1,0:T(8,128)(2,1)} async-done(((bf16[1024,768]{1,0:T(8,128)(2,1)}), bf16[4096,768]{1,0:T(8,128)(2,1)}) %all-gather.8.cloned.1.call-update) | async-done | bytes 6291472 | tf_op jit(solution)/shard_map/all_gather | solution.py:164
  471.6 34.9 %multiply_convert_fusion.1 = (bf16[4096,768]{1,0:T(8,128)(2,1)}, f32[4096,768]{1,0:T(8,128)}, f32[4096,768]{1,0:T(8,128)}) fusion(f32[768]{0:T(1024)S(1)} %convert_element_type.114, bf16[4096,768]{1,0:T(8,128)(2,1)} %all-gather.8.cloned.1.call-done, bf16[768,768]{1,0:T(8,128)(2,1)} %all-gather.10.cloned.1.call-done), kind=kOutput, calls=%fused_computation.62 | convolution fusion | flops 5039456256 | bytes 38931456 | tf_op jit(solution)/shard_map/dot_general | solution.py:13
  506.4 8.6 all-gather.12.cloned.1.call-done
  515.0 9.2 convolution_convert_fusion.2
  525.0 56.1 %reduce-scatter.11.cloned.1.call-done = bf16[1024,768]{1,0:T(8,128)(2,1)} async-done(((bf16[4096,768]{1,0:T(8,128)(2,1)}), bf16[1024,768]{1,0:T(8,128)(2,1)}) %reduce-scatter.11.cloned.1.call-update) | async-done | bytes 1572880 | tf_op jit(solution)/shard_map/reduce_scatter | solution.py:170
  591.7 19.8 %collective-permute-done = bf16[1024,768]{1,0:T(8,128)(2,1)S(1)} collective-permute-done((bf16[1024,768]{1,0:T(8,128)(2,1)S(1)}, bf16[1024,768]{1,0:T(8,128)(2,1)S(1)}, u32[]{:S(2)}, u32[]{:S(2)}) %collective-permute-start) | collective-permute-done | bytes 1572896 | tf_op jit(solution)/shard_map/ppermute | solution.py:189
  612.6 19.9 %collective-permute-done.1 = bf16[1024,768]{1,0:T(8,128)(2,1)} collective-permute-done((bf16[1024,768]{1,0:T(8,128)(2,1)S(1)}, bf16[1024,768]{1,0:T(8,128)(2,1)}, u32[]{:S(2)}, u32[]{:S(2)}) %collective-permute-start.1) | collective-permute-done | bytes 1572896 | tf_op jit(solution)/shard_map/ppermute | solution.py:189
  632.6 20.1 %collective-permute-done.2 = bf16[1024,768]{1,0:T(8,128)(2,1)} collective-permute-done((bf16[1024,768]{1,0:T(8,128)(2,1)}, bf16[1024,768]{1,0:T(8,128)(2,1)}, u32[]{:S(2)}, u32[]{:S(2)}) %collective-permute-start.2) | collective-permute-done | bytes 1572896 | tf_op jit(solution)/shard_map/ppermute | solution.py:189
  663.9 18.3 %convert_reduce_fusion = (f32[768]{0:T(1024)}, bf16[4096,768]{1,0:T(8,128)(2,1)}) fusion(f32[4096,768]{1,0:T(8,128)} %get-tuple-element.388, bf16[768,768]{1,0:T(8,128)(2,1)S(1)} %copy-done.46, bf16[8192,768]{1,0:T(8,128)(2,1)} %copy-done.28, s32[]{:T(128)S(6)} %select_n.33, f32[4096,768]{1,0:T(8,128)} %get-tuple-element.404, f32[768]{0:T(1024)S(1)} %convert_element_type.114), kind=kOutput, calls=%fused_computation.60 | convolution fusion | flops 4885314560 | bytes 38934532 | tf_op jit(solution)/shard_map/dot_general | solution.py:13
  682.1 9.7 convolution_convert_fusion.1
  691.9 58.3 %reduce-scatter.13.cloned.1.call-done = bf16[1024,768]{1,0:T(8,128)(2,1)} async-done(((bf16[4096,768]{1,0:T(8,128)(2,1)}), bf16[1024,768]{1,0:T(8,128)(2,1)}) %reduce-scatter.13.cloned.1.call-update) | async-done | bytes 1572880 | tf_op jit(solution)/shard_map/reduce_scatter | solution.py:200
  757.9 46.5 %all-gather.14.cloned.1.call-done = bf16[4096,768]{1,0:T(8,128)(2,1)} async-done(((bf16[1024,768]{1,0:T(8,128)(2,1)}), bf16[4096,768]{1,0:T(8,128)(2,1)}) %all-gather.14.cloned.1.call-update) | async-done | bytes 6291472 | tf_op jit(solution)/shard_map/all_gather | solution.py:211
  815.2 383.9 %while.56 = (s32[]{:T(128)}, bf16[2,2048,3,64]{3,2,1,0:T(4,128)(2,1)}, bf16[2,2048,3,64]{1,3,2,0:T(8,128)(2,1)}, bf16[2,2048,3,64]{1,3,2,0:T(8,128)(2,1)}, bf16[...) while((s32[]{:T(128)}, ...), condition=%wide.region_21.22_spmd, body=%wide.region_17.21_spmd.sunk | while | flops 2063563264 | bytes 214689712 | solution.py:220
  823.5 177.1 %while.58 = (s32[]{:T(128)}, f32[2048,3,64]{0,2,1:T(8,128)}, f32[2048,3,64]{0,2,1:T(8,128)}, bf16[4,512,3,64]{1,3,2,0:T(8,128)(2,1)}, s32[4]{0:T(128)S(1)}, /*in...) while((s32[]{:T(128)}, f32[2048,3,64]{0,2,1:T(8,128)}, ...), condition=%wide.region_20.20_spmd.clone, body=%wide.region_18.19_spmd.clone.sunk | while | flops 2063563264 | bytes 194437712 | solution.py:104
  835.0 7.9 multiply_reduce_fusion.7
  857.5 9.7 fusion.129
  878.6 7.9 multiply_reduce_fusion.7
  901.5 10.1 fusion.129
  923.1 7.9 multiply_reduce_fusion.7
  946.0 10.1 fusion.129
  967.5 7.9 multiply_reduce_fusion.7
  990.5 10.1 fusion.129
  1015.3 177.1 %while.58 = (s32[]{:T(128)}, f32[2048,3,64]{0,2,1:T(8,128)}, f32[2048,3,64]{0,2,1:T(8,128)}, bf16[4,512,3,64]{1,3,2,0:T(8,128)(2,1)}, s32[4]{0:T(128)S(1)}, /*in...) while((s32[]{:T(128)}, f32[2048,3,64]{0,2,1:T(8,128)}, ...), condition=%wide.region_20.20_spmd.clone, body=%wide.region_18.19_spmd.clone.sunk | while | flops 2063563264 | bytes 194437712 | solution.py:104
  1026.7 7.9 multiply_reduce_fusion.7
  1049.2 9.7 fusion.129
  1070.4 7.9 multiply_reduce_fusion.7
  1093.3 10.1 fusion.129
  1114.8 7.9 multiply_reduce_fusion.7
  1137.8 10.1 fusion.129
  1159.3 7.9 multiply_reduce_fusion.7
  1182.3 10.1 fusion.129
  1199.1 9.8 copy.67
  1216.7 7.1 convolution_convert_fusion
  1223.8 10.1 fusion.42
  1234.0 11.2 fusion.70
  1251.2 7.5 fusion.68
  1260.9 41.0 %psum.23 = f32[6,768]{1,0:T(8,128)} all-reduce(f32[6,768]{1,0:T(8,128)S(1)} %stack.39), channel_id=1, replica_groups=mesh['dp'=8,'tensor'=4] {'dp','tensor'}, use_global_device_ids=true, to_apply=%region_38.39 | all-reduce | flops 4608 | bytes 36864 | tf_op jit(solution)/shard_map/psum | solution.py:252
  1306.3 22.5 %all-reduce = (f32[2,192]{1,0:T(2,128)}, f32[768]{0:T(1024)}) all-reduce(f32[2,192]{1,0:T(2,128)S(1)} %pad_maximum_fusion, f32[768]{0:T(1024)S(1)} %copy-done.36), channel_id=1, replica_groups=mesh['dp'=8,'tensor'=4] {'dp'}, use_global_device_ids=true, to_apply=%region_26.27 | all-reduce | flops 1152 | bytes 9216 | tf_op jit(solution)/shard_map/psum | solution.py:251
  1332.2 24.6 %reduce-scatter.23.cloned.1.call-done = f32[96,768]{1,0:T(8,128)} async-done(((f32[768,768]{1,0:T(8,128)}), f32[96,768]{1,0:T(8,128)}) %reduce-scatter.23.cloned.1.call-update) | async-done | bytes 294928 | tf_op jit(solution)/shard_map/reduce_scatter | solution.py:249
  1356.8 72.4 %reduce-scatter.21.cloned.1.call-done = f32[96,768]{1,0:T(8,128)} async-done(((f32[768,768]{1,0:T(8,128)}), f32[96,768]{1,0:T(8,128)}) %reduce-scatter.21.cloned.1.call-update) | async-done | bytes 294928 | tf_op jit(solution)/shard_map/reduce_scatter | solution.py:248
  1429.2 65.7 %reduce-scatter.19.cloned.1.call-done = f32[96,192]{1,0:T(8,128)} async-done(((f32[768,192]{1,0:T(8,128)}), f32[96,192]{1,0:T(8,128)}) %reduce-scatter.19.cloned.1.call-update) | async-done | bytes 73744 | tf_op jit(solution)/shard_map/reduce_scatter | solution.py:247
  1494.9 72.2 %reduce-scatter.17.cloned.1.call-done = f32[96,3,192]{2,0,1:T(8,128)} async-done(((f32[768,3,192]{2,0,1:T(8,128)}), f32[96,3,192]{2,0,1:T(8,128)}) %reduce-scatter.17.cloned.1.call-update) | async-done | bytes 221200 | tf_op jit(solution)/shard_map/reduce_scatter | solution.py:246
  (519 shorter events, 412.1 us)
Async XLA Ops:
  8.0 41.6 %copy-start.29 = (bf16[96,192]{1,0:T(8,128)(2,1)S(1)}, bf16[96,192]{1,0:T(8,128)(2,1)}, u32[]{:S(2)}) copy-start(bf16[96,192]{1,0:T(8,128)(2,1)} %param.27) | copy-start | bytes 110596
  8.0 74.7 %copy-start.37 = (bf16[2,192]{1,0:T(2,128)(2,1)S(1)}, bf16[2,192]{1,0:T(2,128)(2,1)}, u32[]{:S(2)}) copy-start(bf16[2,192]{1,0:T(2,128)(2,1)} %param.26) | copy-start | bytes 2308
  8.0 74.7 %all-gather.6.cloned.1.call-start = ((), (), s32[]{:S(2)}) async-start(), calls=%async_computation.8 | async-start | bytes 7864320 | tf_op jit(solution)/shard_map/all_gather | solution.py:130
  8.8 411.4 %reduce-scatter.9.cloned.1.call-start = ((), (), s32[]{:S(2)}) async-start(), calls=%async_computation.9 | async-start | bytes 15728640 | tf_op jit(solution)/shard_map/reduce_scatter | solution.py:153
  49.6 39.2 %copy-start.24 = (bf16[768,3,192]{0,2,1:T(8,128)(2,1)}, bf16[768,3,192]{0,2,1:T(8,128)(2,1)S(1)}, u32[]{:S(2)}) copy-start(bf16[768,3,192]{0,2,1:T(8,128)(2,1)S(1)} %copy.56) | copy-start | bytes 2654212
  303.6 18.2 %copy-start.26 = (f32[2,4,3,512]{3,2,1,0:T(4,128)}, f32[2,4,3,512]{3,2,1,0:T(4,128)S(1)}, u32[]{:S(2)}) copy-start(f32[2,4,3,512]{3,2,1,0:T(4,128)S(1)} %get-tuple-element.826) | copy-start | bytes 147460
  303.6 11.8 copy-start.20
  321.9 104.0 %all-gather.10.cloned.1.call-start = ((), (), s32[]{:S(2)}) async-start(), calls=%async_computation.11 | async-start | bytes 1327104 | tf_op jit(solution)/shard_map/all_gather | solution.py:134
  322.5 149.1 %all-gather.8.cloned.1.call-start = ((), (), s32[]{:S(2)}) async-start(), calls=%async_computation.10 | async-start | bytes 7864320 | tf_op jit(solution)/shard_map/all_gather | solution.py:164
  425.2 89.8 %all-gather.12.cloned.1.call-start = ((), (), s32[]{:S(2)}) async-start(), calls=%async_computation.12 | async-start | bytes 1327104 | tf_op jit(solution)/shard_map/all_gather | solution.py:135
  425.8 155.3 %reduce-scatter.11.cloned.1.call-start = ((), (), s32[]{:S(2)}) async-start(), calls=%async_computation.13 | async-start | bytes 7864320 | tf_op jit(solution)/shard_map/reduce_scatter | solution.py:170
  524.3 226.0 %reduce-scatter.13.cloned.1.call-start = ((), (), s32[]{:S(2)}) async-start(), calls=%async_computation.14 | async-start | bytes 7864320 | tf_op jit(solution)/shard_map/reduce_scatter | solution.py:200
  591.6 19.8 %collective-permute-start = (bf16[1024,768]{1,0:T(8,128)(2,1)S(1)}, bf16[1024,768]{1,0:T(8,128)(2,1)S(1)}, u32[]{:S(2)}, u32[]{:S(2)}) collective-permute-start(bf16[1024,768]{1,0:T(8,128)(2,1)S(1)} %get-tuple-element.380), channel_id=1, source_target_pairs={{0,1},{1,2},{2,3},{3,0},{4,5},{5,6},{6,7},{7,4},{8,9},{9,10},{10,1... | collective-permute-start | bytes 4718600 | tf_op jit(solution)/shard_map/ppermute | solution.py:189
  612.6 19.9 %collective-permute-start.1 = (bf16[1024,768]{1,0:T(8,128)(2,1)S(1)}, bf16[1024,768]{1,0:T(8,128)(2,1)}, u32[]{:S(2)}, u32[]{:S(2)}) collective-permute-start(bf16[1024,768]{1,0:T(8,128)(2,1)S(1)} %collective-permute-done), channel_id=1, source_target_pairs={{0,1},{1,2},{2,3},{3,0},{4,5},{5,6},{6,7},{7,4},{8,9},{9,10},{10,1... | collective-permute-start | bytes 4718600 | tf_op jit(solution)/shard_map/ppermute | solution.py:189
  632.6 20.2 %collective-permute-start.2 = (bf16[1024,768]{1,0:T(8,128)(2,1)}, bf16[1024,768]{1,0:T(8,128)(2,1)}, u32[]{:S(2)}, u32[]{:S(2)}) collective-permute-start(bf16[1024,768]{1,0:T(8,128)(2,1)} %collective-permute-done.1), channel_id=1, source_target_pairs={{0,1},{1,2},{2,3},{3,0},{4,5},{5,6},{6,7},{7,4},{8,9},{9,10},{10,1... | collective-permute-start | bytes 4718600 | tf_op jit(solution)/shard_map/ppermute | solution.py:189
  632.6 23.2 %copy-start.17 = (bf16[1024,768]{1,0:T(8,128)(2,1)S(1)}, bf16[1024,768]{1,0:T(8,128)(2,1)}, u32[]{:S(2)}) copy-start(bf16[1024,768]{1,0:T(8,128)(2,1)} %copy-done.16) | copy-start | bytes 4718596
  632.6 23.3 %copy-start.11 = (bf16[1024,768]{1,0:T(8,128)(2,1)S(1)}, bf16[1024,768]{1,0:T(8,128)(2,1)}, u32[]{:S(2)}) copy-start(bf16[1024,768]{1,0:T(8,128)(2,1)} %copy-done.10) | copy-start | bytes 4718596
  663.9 18.3 %copy-start.45 = (bf16[768,768]{1,0:T(8,128)(2,1)S(1)}, bf16[768,768]{1,0:T(8,128)(2,1)}, u32[]{:S(2)}) copy-start(bf16[768,768]{1,0:T(8,128)(2,1)} %all-gather.10.cloned.1.call-done) | copy-start | bytes 3538948
  691.9 112.5 %all-gather.14.cloned.1.call-start = ((), (), s32[]{:S(2)}) async-start(), calls=%async_computation.15 | async-start | bytes 7864320 | tf_op jit(solution)/shard_map/all_gather | solution.py:211
  754.3 50.1 %copy-start.21 = (bf16[768,192]{1,0:T(8,128)(2,1)S(1)}, bf16[768,192]{1,0:T(8,128)(2,1)}, u32[]{:S(2)}) copy-start(bf16[768,192]{1,0:T(8,128)(2,1)} %all_gather.23) | copy-start | bytes 884740
  757.9 570.9 %reduce-scatter.15.cloned.1.call-start = ((), (), s32[]{:S(2)}) async-start(), calls=%async_computation.16 | async-start | bytes 7864320 | tf_op jit(solution)/shard_map/reduce_scatter | solution.py:239
  834.9 8.0 slice-start
  834.9 8.0 slice-start.1
  834.9 8.8 slice-start.2
  857.4 9.7 copy-start.8
  857.4 9.7 copy-start.5
  878.6 8.0 slice-start
  878.6 8.0 slice-start.1
  878.6 8.8 slice-start.2
  901.5 10.2 copy-start.8
  901.5 10.1 copy-start.5
  923.0 8.0 slice-start
  923.0 8.0 slice-start.1
  923.1 8.8 slice-start.2
  946.0 10.2 copy-start.8
  946.0 10.1 copy-start.5
  967.5 8.8 slice-start.2
  990.5 10.2 copy-start.8
  990.5 10.1 copy-start.5
  1026.7 8.0 slice-start
  1026.7 8.0 slice-start.1
  1026.7 8.8 slice-start.2
  1049.2 9.7 copy-start.8
  1049.2 9.7 copy-start.5
  1070.3 8.0 slice-start
  1070.3 8.0 slice-start.1
  1070.3 8.8 slice-start.2
  1093.3 10.2 copy-start.8
  1093.3 10.1 copy-start.5
  1114.8 8.0 slice-start
  1114.8 8.0 slice-start.1
  1114.8 8.8 slice-start.2
  1137.7 10.2 copy-start.8
  1137.7 10.1 copy-start.5
  1159.3 8.8 slice-start.2
  1182.2 10.2 copy-start.8
  1182.2 10.1 copy-start.5
  1199.1 10.6 copy-start.22
  1223.7 133.0 %reduce-scatter.23.cloned.1.call-start = ((), (), s32[]{:S(2)}) async-start(), calls=%async_computation.20 | async-start | bytes 2654208 | tf_op jit(solution)/shard_map/reduce_scatter | solution.py:249
  1233.9 11.3 copy-start.15
  1233.9 195.3 %reduce-scatter.21.cloned.1.call-start = ((), (), s32[]{:S(2)}) async-start(), calls=%async_computation.19 | async-start | bytes 2654208 | tf_op jit(solution)/shard_map/reduce_scatter | solution.py:248
  1245.2 249.7 %reduce-scatter.19.cloned.1.call-start = ((), (), s32[]{:S(2)}) async-start(), calls=%async_computation.18 | async-start | bytes 884736 | tf_op jit(solution)/shard_map/reduce_scatter | solution.py:247
  1251.2 316.0 %reduce-scatter.17.cloned.1.call-start = ((), (), s32[]{:S(2)}) async-start(), calls=%async_computation.17 | async-start | bytes 2654208 | tf_op jit(solution)/shard_map/reduce_scatter | solution.py:246
  1305.6 23.2 %copy-start.12 = (f32[1024,768]{1,0:T(8,128)S(1)}, f32[1024,768]{1,0:T(8,128)}, u32[]{:S(2)}) copy-start(f32[1024,768]{1,0:T(8,128)} %get-tuple-element.384) | copy-start | bytes 9437188
  (80 other events, 376.8 us)
Sparse Core Ops, SparseCore 0:
  10.4 49.0 all-gather.5
  322.0 98.1 reduce-scatter.8
  758.0 46.3 all-gather.13
Sparse Core Ops, SparseCore 1:
  324.5 40.6 all-gather.9
  425.3 46.2 all-gather.7
  473.6 41.3 all-gather.11
  524.4 56.7 reduce-scatter.10
  692.0 58.2 reduce-scatter.12
  1223.8 58.9 reduce-scatter.14
  1287.1 69.6 reduce-scatter.22
  1361.1 68.0 reduce-scatter.20
  1433.3 61.6 reduce-scatter.18
  1499.0 68.1 reduce-scatter.16
